TPU v7x, 32 devices: a whole 2x2x4 slice. The times are simulated.
32 devices in a mesh: survey: 2 (over x), chan: 16 (over z, y, core).
Axes of the slice: x: 2, y: 2, z: 4, core: 2. Of those that a mesh axis runs over, the one named last changes fastest.
Arguments:
- das_window: float32 [8192, 8192], P(('survey', 'chan')), parts along dimension 0, may hold values from -6 to 6
- fan_bound: int32 [4096], replicated, may hold values from -1 to 2048, as said below
- tap_offset: int32 [8, 32], replicated, may hold values from -31 to 31, as said below
- tap_weight: float32 [8, 32], replicated, may hold values from -1 to 1
Outputs:
- filtered: float32 [8192, 8192], P(('survey', 'chan')), parts along dimension 0
- energy: float32 [8192, 8, 128], P(('survey', 'chan')), parts along dimension 0
There are 2 independent parts, one for each index of `survey`. A program takes and returns all parts, laid end to end along the dimension named above; an argument that names none is the same for every part. Nothing has to cross between parts.
Inputs may be any that keep to these rules, and one draw needn't show every extreme that they name: `fan_bound`: entry f bounds the magnitude of the signed channel wavenumber bin passed at the time frequency bins +f and -f; -1 passes none. `tap_offset`: the channel offset of a tap relative to the output channel.
All inputs are finite; a program needn't handle non-finite values.
Results may differ from a plain program's by a relative error of at most 0.0027.
Values may be sent and summed in bfloat16 or wider, within the bound.
No kernel may reach another device: no remote copies, remote signals or barrier semaphores. Data moves between devices by JAX's collectives and lax.ppermute only.
A program may use at most 256 MiB of HBM per device.

v0:
```python
import math

import jax
import jax.numpy as jnp
from jax import lax
from jax.sharding import PartitionSpec as P

HALO = 31
WIN = 64


PRECISE = lax.Precision.HIGHEST


def padded_2(value, sides, width):
    for axis, dim in sides:
        peers, length = (lax.axis_size(axis), value.shape[dim])
        up = [(i, (i + 1) % peers) for i in range(peers - 1)]
        down = [(j, i) for i, j in up]
        last = lax.slice_in_dim(value, length - width, length, axis=dim)
        leading = lax.slice_in_dim(value, 0, width, axis=dim)
        before = lax.ppermute(last, axis, up)
        after = lax.ppermute(leading, axis, down)
        value = jnp.concatenate([before, value, after], axis=dim)
    return value


def split_length(length_all):
    leading = 1
    while length_all % (4 * leading) == 0 and 4 * leading * leading <= length_all:
        leading = leading * 2
    return (leading, length_all // leading)


def phases(index_product, modulus, direction):
    angle = (index_product % modulus).astype(jnp.float32) * (2.0 * math.pi / modulus)
    return (jnp.cos(angle), direction * jnp.sin(angle))


def complex_table(real_part, imag_part, q_axis):
    first_row = jnp.stack([real_part, imag_part], axis=q_axis)
    second_row = jnp.stack([-imag_part, real_part], axis=q_axis)
    return jnp.stack([first_row, second_row], axis=0)


def square_phases(leading, direction):
    left_index = lax.broadcasted_iota(jnp.int32, (leading, leading), 0)
    right_index = lax.broadcasted_iota(jnp.int32, (leading, leading), 1)
    return phases(left_index * right_index, leading, direction)


def folded_table(shape_three, bin_axis, inner_axis, leading, modulus, direction):
    bin_index = lax.broadcasted_iota(jnp.int32, shape_three, bin_axis)
    outer_index = lax.broadcasted_iota(jnp.int32, shape_three, 3 - bin_axis - inner_axis)
    inner_index = lax.broadcasted_iota(jnp.int32, shape_three, inner_axis)
    return phases(inner_index * (bin_index + leading * outer_index), modulus, direction)


def time_forward(signal, kept_bins):
    row_count, sample_count = signal.shape
    leading, trailing = split_length(sample_count)
    used_bins = kept_bins // leading
    shaped = signal.reshape(row_count, leading, trailing)
    cos_first, sin_first = square_phases(leading, -1.0)
    first_table = jnp.stack([cos_first, sin_first], axis=1)
    first = jnp.einsum("rab,apk->rpkb", shaped, first_table, precision=PRECISE)
    cos_second, sin_second = folded_table(
        (leading, trailing, used_bins), 0, 1, leading, sample_count, -1.0
    )
    second_table = complex_table(cos_second, sin_second, 2)
    out = jnp.einsum("rpkb,pkbqm->rqmk", first, second_table, precision=PRECISE)
    return out.reshape(row_count, 2, kept_bins)


def channel_transform(field, direction):
    length_all, parts_count, column_count = field.shape
    leading, trailing = split_length(length_all)
    shaped = field.reshape(leading, trailing, parts_count, column_count)
    cos_first, sin_first = square_phases(leading, direction)
    first_table = complex_table(cos_first, sin_first, 1)
    first = jnp.einsum("abpn,paqk->kbqn", shaped, first_table, precision=PRECISE)
    cos_second, sin_second = folded_table(
        (leading, trailing, trailing), 0, 1, leading, length_all, direction
    )
    second_table = complex_table(cos_second, sin_second, 2)
    out = jnp.einsum("kbpn,pkbqm->mkqn", first, second_table, precision=PRECISE)
    return out.reshape(length_all, parts_count, column_count)


def time_inverse(spectrum, sample_count):
    row_count, parts_count, bin_count = spectrum.shape
    leading, trailing = split_length(sample_count)
    used_bins = bin_count // leading
    shaped = spectrum.reshape(row_count, parts_count, used_bins, leading)
    cos_first, sin_first = folded_table(
        (leading, used_bins, trailing), 0, 2, leading, sample_count, 1.0
    )
    first_table = complex_table(cos_first, sin_first, 2)
    first = jnp.einsum("rpmk,pkmqb->rqkb", shaped, first_table, precision=PRECISE)
    cos_last, sin_last = square_phases(leading, 1.0)
    last_table = jnp.stack([cos_last, -sin_last], axis=0)
    signal = jnp.einsum("rqkb,qka->rab", first, last_table, precision=PRECISE)
    signal = signal.reshape(row_count, sample_count)
    signal = 2.0 * signal - spectrum[:, 0, 0:1]
    return signal / sample_count


def per_device(das_window, fan_bound, tap_offset, tap_weight):
    row_count, sample_count = das_window.shape
    devices = lax.axis_size("chan")
    channel_count = row_count * devices
    kept_bins = sample_count // 2
    block_bins = kept_bins // devices
    spectrum = time_forward(das_window, kept_bins)
    by_freq = lax.all_to_all(spectrum, "chan", split_axis=2, concat_axis=0, tiled=True)
    wave = channel_transform(by_freq, -1.0)
    wave_index = lax.broadcasted_iota(jnp.int32, (channel_count, 1), 0)
    wave_signed = jnp.where(wave_index < channel_count // 2, wave_index, wave_index - channel_count)
    position = lax.axis_index("chan")
    extended = jnp.concatenate([fan_bound, jnp.full((1,), -1, jnp.int32)])
    limits = lax.dynamic_slice_in_dim(extended, position * block_bins, block_bins)
    passing = (jnp.abs(wave_signed) <= limits[None, :]).astype(jnp.float32)
    back = channel_transform(wave * passing[:, None, :], 1.0) / channel_count
    by_channel = lax.all_to_all(back, "chan", split_axis=0, concat_axis=2, tiled=True)
    filtered = time_inverse(by_channel, sample_count)
    low_field = filtered.astype(jnp.bfloat16)
    padded = padded_2(low_field, (("chan", 0),), HALO)
    span_count = 2 * HALO + 1
    offsets_grid = jnp.arange(span_count, dtype=jnp.int32) - HALO
    matches = (tap_offset[:, :, None] == offsets_grid[None, None, :]).astype(jnp.float32)
    kernel_low = jnp.sum(tap_weight[:, :, None] * matches, axis=1).astype(jnp.bfloat16)
    template_count = kernel_low.shape[0]
    piece_rows = 64
    offset_index = lax.broadcasted_iota(
        jnp.int32, (span_count, piece_rows, piece_rows + 2 * HALO), 0
    )
    output_index = lax.broadcasted_iota(
        jnp.int32, (span_count, piece_rows, piece_rows + 2 * HALO), 1
    )
    input_index = lax.broadcasted_iota(
        jnp.int32, (span_count, piece_rows, piece_rows + 2 * HALO), 2
    )
    selector = (input_index - output_index == offset_index).astype(jnp.bfloat16)
    stacking = jnp.einsum("ko,ori->rki", kernel_low, selector, preferred_element_type=jnp.float32)
    stacking = stacking.astype(jnp.bfloat16).reshape(
        piece_rows * template_count, piece_rows + 2 * HALO
    )

    def one_piece(first_row):
        window_rows = lax.dynamic_slice_in_dim(padded, first_row, piece_rows + 2 * HALO, 0)
        detection = jnp.dot(stacking, window_rows, preferred_element_type=jnp.float32)
        squared = (detection * detection).reshape(
            piece_rows * template_count, sample_count // WIN, WIN
        )
        return jnp.mean(squared, axis=2).reshape(piece_rows, template_count, sample_count // WIN)

    starts = jnp.arange(0, row_count, piece_rows, dtype=jnp.int32)
    energy = lax.map(one_piece, starts).reshape(row_count, template_count, sample_count // WIN)
    return (filtered, energy)


def solution(mesh):
    return jax.shard_map(
        per_device,
        mesh=mesh,
        in_specs=(P(("survey", "chan"), None), P(), P(), P()),
        out_specs=(P(("survey", "chan"), None), P(("survey", "chan"), None, None)),
        check_vma=False,
    )
```

profile of v0, /device:TPU:19, one launch (start us, length us, event | category | flops | bytes accessed | tf_op | source)
XLA Modules:
  0.0 740.4 jit_solution(12700331765586824724)
XLA Ops:
  0.8 8.4 %sine_multiply_fusion = (f32[64,128,1,64]{1,3,2,0:T(8,128)S(1)}, f32[64,128,1,64]{1,3,2,0:T(8,128)S(1)}, f32[64,128,1,64]{1,3,2,0:T(8,128)S(1)}) fusion(s32[64]{0:T(128)S(1)} %iota_multiply_fusion.1), kind=kLoop, calls=%fused_computation.74 | loop fusion | flops 8912896 | bytes 6291712 | tf_op jit(solution)/shard_map/mul | solution.py:37
  9.2 5.0 copy.102
  14.3 4.3 maximum_bitcast_fusion.2
  18.6 16.0 %convolution_bitcast_fusion.1 = f32[256,2,64,128,1]{3,2,0,1,4:T(8,128)} fusion(f32[256,64,128,1]{2,1,0,3:T(8,128)S(1)} %bitcast.148, f32[64,1,64]{0,2,1:T(8,128)S(1)} %get-tuple-element.68, f32[64,1,64]{0,2,1:T(8,128)S(1)} %get-tuple-element.67), kind=kOutput, calls=%fused_computation.37 | convolution fusion | flops 3221233664 | bytes 25198592 | tf_op jit(solution)/shard_map/rab,apk->rpkb/dot_general | solution.py:66
  34.6 33.7 %fusion.37 = f32[256,2,64,64]{0,2,1,3:T(8,128)S(1)} fusion(f32[256,2,64,128,1]{3,2,0,1,4:T(8,128)} %convolution_bitcast_fusion.1, f32[1,64,128,2,64]{2,4,0,3,1:T(8,128)} %get-tuple-element.51, f32[1,64,128,2,64]{2,4,0,3,1:T(8,128)} %get-tuple-element.50), kind=kOutput, calls=%fused_computation.54 | convolution fusion | flops 6444548096 | bytes 33554432 | tf_op jit(solution)/shard_map/rpkb,pkbqm->rqmk/dot_general | solution.py:71
  68.3 4.9 copy.56
  73.1 23.4 %copy.57 = f32[256,2,4096]{0,1,2:T(2,128)} copy(f32[256,2,4096]{0,2,1:T(8,128)S(1)} %bitcast.153) | data formatting | bytes 16777216 | tf_op jit(solution)/shard_map/reshape | solution.py:72
  96.6 6.9 all-to-all-start
  106.2 8.5 %broadcast_multiply_fusion.1 = (f32[64,64,1,64]{1,3,0,2:T(8,128)S(1)}, f32[64,64,1,64]{1,3,0,2:T(8,128)S(1)}, f32[64,64,1,64]{1,3,0,2:T(8,128)S(1)}, f32[64,64,1,64]{1,3,0,2:T(8,128)S(1)}, f32[64,64,1,64]{1,3,0,2:T(8,128)S(1)}) fusion(s32[64]{0:T(128)S(1)} %iota_multiply_fusion.1), kind=kLoop, calls=%fused_computation.83 | loop fusion | flops 4718592 | bytes 5243136 | tf_op jit(solution)/shard_map/mul | solution.py:37
  114.7 7.4 fusion.30
  122.1 163.2 %all-to-all-done = f32[256,2,4096]{0,1,2:T(2,128)} async-done(((f32[256,2,4096]{0,1,2:T(2,128)}), f32[256,2,4096]{0,1,2:T(2,128)}, u32[]{:S(2)}, u32[]{:S(2)}) %all-to-all-start) | async-done | bytes 8388640 | tf_op jit(solution)/shard_map/all_to_all | solution.py:115
  285.3 7.4 %copy.58 = f32[256,2,4096]{0,2,1:T(8,128)} copy(f32[256,2,4096]{0,1,2:T(2,128)} %all-to-all-done) | data formatting | bytes 16777216 | tf_op jit(solution)/shard_map/all_to_all | solution.py:115
  292.7 8.7 %copy.59 = f32[16,256,2,256]{3,1,0,2:T(8,128)} copy(f32[16,256,2,256]{1,3,0,2:T(8,128)} %bitcast.154) | data formatting | bytes 16777216 | tf_op jit(solution)/shard_map/all_to_all | solution.py:115
  301.5 17.6 %fusion.31 = f32[64,64,2,256,1]{3,0,1,2,4:T(8,128)} fusion(f32[64,64,2,256]{3,1,0,2:T(8,128)} %bitcast.152, f32[1,64,2,64]{1,3,2,0:T(8,128)S(1)} %get-tuple-element.53, f32[1,64,2,64]{1,3,2,0:T(8,128)S(1)} %get-tuple-element.54), kind=kOutput, calls=%fused_computation.52 | convolution fusion | flops 3221241856 | bytes 16842752 | tf_op jit(solution)/shard_map/abpn,paqk->kbqn/dot_general | solution.py:81
  319.1 22.0 %fusion.20 = f32[64,2,64,256,1]{3,2,1,0,4:T(8,128)} fusion(f32[64,64,2,256,1]{3,0,1,2,4:T(8,128)} %fusion.31, f32[1,64,64,2,64]{2,4,1,3,0:T(8,128)} %get-tuple-element.47, f32[1,64,64,2,64]{2,4,1,3,0:T(8,128)} %get-tuple-element.46), kind=kOutput, calls=%fused_computation.30 | convolution fusion | flops 3222274048 | bytes 20971520 | tf_op jit(solution)/shard_map/kbpn,pkbqm->mkqn/dot_general | solution.py:86
  341.1 11.9 %fusion.34 = f32[64,64,2,256,1]{3,0,1,2,4:T(8,128)} fusion(f32[64,2,64,256,1]{3,2,1,0,4:T(8,128)} %fusion.20, f32[64,64,256]{2,0,1:T(8,128)S(1)} %copy-done.1, f32[1,64,2,64]{1,3,2,0:T(8,128)S(1)} %get-tuple-element.55, f32[1,64,2,64]{1,3,2,0:T(8,128)S(1)} %get-tuple-element.52), kind=kOutput, calls=%fused_computation.53 | convolution fusion | flops 3223339008 | bytes 21037056 | tf_op jit(solution)/shard_map/abpn,paqk->kbqn/dot_general | solution.py:81
  353.0 22.1 %fusion.8 = f32[64,2,64,256,1]{3,2,0,1,4:T(8,128)} fusion(f32[1,64,64,2,64]{2,4,1,3,0:T(8,128)} %get-tuple-element.48, f32[1,64,64,2,64]{2,4,1,3,0:T(8,128)} %get-tuple-element.49, f32[64,64,2,256,1]{3,0,1,2,4:T(8,128)} %fusion.34), kind=kOutput, calls=%fused_computation.14 | convolution fusion | flops 3222274048 | bytes 20971520 | tf_op jit(solution)/shard_map/kbpn,pkbqm->mkqn/dot_general | solution.py:86
  375.2 4.3 fusion.16
  379.4 4.9 copy.67
  384.3 23.4 %copy.68 = f32[4096,2,256]{2,1,0:T(2,128)} copy(f32[4096,2,256]{2,0,1:T(8,128)S(1)} %bitcast.155) | data formatting | bytes 16777216 | tf_op jit(solution)/shard_map/div | solution.py:123
  407.7 5.2 all-to-all-start.1
  413.1 8.4 %fusion.55 = (f32[64,64,1,128]{3,1,2,0:T(8,128)S(1)}, f32[64,64,1,128]{3,1,2,0:T(8,128)S(1)}, f32[64,64,1,128]{3,1,2,0:T(8,128)S(1)}) fusion(s32[64]{0:T(128)S(1)} %iota_multiply_fusion.1), kind=kLoop, calls=%fused_computation.79 | loop fusion | flops 8388608 | bytes 6291712 | tf_op jit(solution)/shard_map/sin | solution.py:37
  425.7 169.2 %all-to-all-done.1 = f32[4096,2,256]{2,1,0:T(2,128)} async-done(((f32[4096,2,256]{2,1,0:T(2,128)}), f32[4096,2,256]{2,1,0:T(2,128)}, u32[]{:S(2)}, u32[]{:S(2)}) %all-to-all-start.1) | async-done | bytes 8388640 | tf_op jit(solution)/shard_map/all_to_all | solution.py:124
  594.9 7.4 %copy.69 = f32[4096,2,256]{2,0,1:T(8,128)} copy(f32[4096,2,256]{2,1,0:T(2,128)} %all-to-all-done.1) | data formatting | bytes 16777216 | tf_op jit(solution)/shard_map/all_to_all | solution.py:124
  602.3 8.7 %copy.70 = f32[256,2,16,256]{0,3,2,1:T(8,128)} copy(f32[256,2,16,256]{3,0,2,1:T(8,128)} %bitcast.156) | data formatting | bytes 16777216 | tf_op jit(solution)/shard_map/all_to_all | solution.py:124
  611.0 31.8 %convolution_bitcast_fusion = f32[256,2,64,128]{0,3,1,2:T(8,128)} fusion(f32[1,64,64,2,128]{4,2,0,3,1:T(8,128)} %get-tuple-element.45, f32[1,64,64,2,128]{4,2,0,3,1:T(8,128)} %get-tuple-element.44, f32[256,2,64,64,1]{0,3,2,1,4:T(8,128)} %bitcast.149), kind=kOutput, calls=%fused_computation.8 | convolution fusion | flops 6444548096 | bytes 33554432 | tf_op jit(solution)/shard_map/rpmk,pkmqb->rqkb/dot_general | solution.py:99
  642.8 16.8 %copy.72 = f32[256,2,64,128]{3,2,1,0:T(8,128)} copy(f32[256,2,64,128]{0,3,1,2:T(8,128)} %convolution_bitcast_fusion) | data formatting | bytes 33554432 | tf_op jit(solution)/shard_map/rpmk,pkmqb->rqkb/transpose | solution.py:99
  660.3 12.2 %bitcast_multiply_fusion.1 = f32[64,256,128]{2,0,1:T(8,128)S(1)} fusion(f32[256,2,64,128]{3,2,1,0:T(8,128)} %copy.72, f32[1,64,64]{1,2,0:T(8,128)S(1)} %get-tuple-element.71, f32[1,64,64]{1,2,0:T(8,128)S(1)} %get-tuple-element.72), kind=kOutput, calls=%fused_computation.23 | convolution fusion | flops 3223330816 | bytes 25198592 | tf_op jit(solution)/shard_map/rqkb,qka->rab/dot_general | solution.py:102
  672.5 11.9 %fusion.98 = (bf16[256,8192]{1,0:T(8,128)(2,1)S(1)}, f32[256,8192]{1,0:T(8,128)}) fusion(f32[256]{0:T(256)S(1)} %bitcast.158, f32[32,8,64,128]{3,2,1,0:T(8,128)S(1)} %bitcast.151), kind=kLoop, calls=%fused_computation.144 | loop fusion | flops 6291456 | bytes 20972544 | tf_op jit(solution)/shard_map/convert_element_type | solution.py:126
  692.1 8.4 %collective-permute-done = bf16[31,8192]{1,0:T(8,128)(2,1)S(1)} collective-permute-done((bf16[31,8192]{1,0:T(8,128)(2,1)S(1)}, bf16[31,8192]{1,0:T(8,128)(2,1)S(1)}, u32[]{:S(2)}, u32[]{:S(2)}) %collective-permute-start) | collective-permute-done | bytes 507936 | tf_op jit(solution)/shard_map/ppermute | solution.py:22
  703.9 6.4 pad_maximum_fusion.1
  710.3 29.7 %while.10 = (s32[]{:T(128)}, f32[4,64,8,128]{3,2,1,0:T(8,128)}, s32[4]{0:T(128)S(1)}, bf16[318,8192]{1,0:T(8,128)(2,1)}, bf16[512,126]{1,0:T(8,128)(2,1)S(1)}, /*index=5*/s32[]{:T(128)}, s32[]{:T(128)}, s32[]{:T(128)}) while((s32[]{:T(128)}, f32[4,64,8,128]{3,2,1,0:T(8,128)}, s32[4]{0:T(128)S(1)}, bf16[318,8192]{1,0:T(8,128)(2,1)}, ...), condition=%wide.region_3.4_spmd, body=%wide.region_1.3_spmd.sunk | while | flops 1065353216 | bytes 4061831 | solution.py:158
  (50 shorter events, 41.1 us)
Async XLA Ops:
  96.6 6.9 copy-start.2
  96.6 188.7 %all-to-all-start = ((f32[256,2,4096]{0,1,2:T(2,128)}), f32[256,2,4096]{0,1,2:T(2,128)}, u32[]{:S(2)}, u32[]{:S(2)}) async-start(f32[256,2,4096]{0,1,2:T(2,128)} %copy.57), calls=%async_computation | async-start | bytes 16777216 | tf_op jit(solution)/shard_map/all_to_all | solution.py:115
  319.1 22.1 %copy-start.1 = (f32[64,64,256]{2,0,1:T(8,128)S(1)}, f32[64,64,256]{2,0,1:T(8,128)}, u32[]{:S(2)}) copy-start(f32[64,64,256]{2,0,1:T(8,128)} %compare_convert_fusion) | copy-start | bytes 12582916
  407.7 187.1 %all-to-all-start.1 = ((f32[4096,2,256]{2,1,0:T(2,128)}), f32[4096,2,256]{2,1,0:T(2,128)}, u32[]{:S(2)}, u32[]{:S(2)}) async-start(f32[4096,2,256]{2,1,0:T(2,128)} %copy.68), calls=%async_computation.1 | async-start | bytes 16777216 | tf_op jit(solution)/shard_map/all_to_all | solution.py:124
  672.5 18.9 %copy-start.3 = (f32[8,32]{1,0:T(8,128)S(1)}, f32[8,32]{1,0:T(8,128)}, u32[]{:S(2)}) copy-start(f32[8,32]{1,0:T(8,128)} %param.9) | copy-start | bytes 3076
  672.5 18.9 %copy-start.4 = (s32[8,32]{1,0:T(8,128)S(1)}, s32[8,32]{1,0:T(8,128)}, u32[]{:S(2)}) copy-start(s32[8,32]{1,0:T(8,128)} %param.8) | copy-start | bytes 3076
  684.4 2.0 copy-start
  686.6 13.9 %collective-permute-start = (bf16[31,8192]{1,0:T(8,128)(2,1)S(1)}, bf16[31,8192]{1,0:T(8,128)(2,1)S(1)}, u32[]{:S(2)}, u32[]{:S(2)}) collective-permute-start(bf16[31,8192]{1,0:T(8,128)(2,1)S(1)} %get-tuple-element.42), channel_id=1, source_target_pairs={{0,1},{1,2},{2,3},{3,4},{4,5},{5,6},{6,7},{7,8},{8,9},{9,10},{10,1... | collective-permute-start | bytes 1523720 | tf_op jit(solution)/shard_map/ppermute | solution.py:22
  688.7 15.2 %collective-permute-start.1 = (bf16[31,8192]{1,0:T(8,128)(2,1)S(1)}, bf16[31,8192]{1,0:T(8,128)(2,1)S(1)}, u32[]{:S(2)}, u32[]{:S(2)}) collective-permute-start(bf16[31,8192]{1,0:T(8,128)(2,1)S(1)} %get-tuple-element.43), channel_id=1, source_target_pairs={{1,0},{2,1},{3,2},{4,3},{5,4},{6,5},{7,6},{8,7},{9,8},{10,9},{11,1... | collective-permute-start | bytes 1523720 | tf_op jit(solution)/shard_map/ppermute | solution.py:23
where the time goes:
time: 750 us; the launch traced here: 740 us
  waiting for transfers between devices  344 us (46%)
  matrix products  184 us (25%)
  local copies, waits for them, and re-layouts  120 us (16%)
  other arithmetic  67 us (9%)
  starting transfers between devices  16.9 us (2%)
  loops' own time  7.54 us (1%)
    all_to_all x1, waiting for transfers between devices, per_device(): lax.all_to_all(back, 'chan', split_axis=0, concat_axis=2, tiled=True)  169 us
    all_to_all x1, waiting for transfers between devices, per_device(): lax.all_to_all(spectrum, 'chan', split_axis=2, concat_axis=0, tiled=True)  163 us
    dot_general x2, matrix products, channel_transform(): out = jnp.einsum('kbpn,pkbqm->mkqn', first, second_table, precision=PRECISE)  44.2 us
    dot_general x1, matrix products, time_forward(): out = jnp.einsum('rpkb,pkbqm->rqmk', first, second_table, precision=PRECISE)  33.7 us
    dot_general x1, matrix products, time_inverse(): jnp.einsum('rpmk,pkmqb->rqkb', shaped, first_table, precision=PRECISE)  31.8 us
    dot_general x2, matrix products, channel_transform(): jnp.einsum('abpn,paqk->kbqn', shaped, first_table, precision=PRECISE)  29.5 us
    div x2, local copies, waits for them, and re-layouts, per_device(): back = channel_transform(wave * passing[:, None, :], 1.0) / channel_count  28.3 us
    reshape x1, local copies, waits for them, and re-layouts, time_forward(): return out.reshape(row_count, 2, kept_bins)  23.4 us
  transfers between devices with their start and end apart: 4, of which 4 were waited for; matrix products, arithmetic and copies ran while one was open for 4% of the time, Pallas kernels for 0%

commit v1 on v0

v1 whole, which is shorter than its diff:
```python
import math
import jax
import jax.numpy as jnp
import numpy as np
from jax import lax
from jax.experimental import pallas as pl
from jax.experimental.pallas import tpu as pltpu
from jax.sharding import PartitionSpec as P

HALO = 31
EDGE = 32
WIN = 64
LANES = 128
BF = jnp.bfloat16
F32 = jnp.float32
VMEM_BYTES = 58 * 1024 * 1024


def cadd(x, y):
    return (x[0] + y[0], x[1] + y[1])


def csub(x, y):
    return (x[0] - y[0], x[1] - y[1])


def cmul_const(x, angle_num, angle_den):
    num = angle_num % angle_den
    if num == 0:
        return x
    if 2 * num == angle_den:
        return (-x[0], -x[1])
    if 4 * num == angle_den:
        return (-x[1], x[0])
    if 4 * num == 3 * angle_den:
        return (x[1], -x[0])
    theta = 2.0 * math.pi * num / angle_den
    c, s = math.cos(theta), math.sin(theta)
    if (8 * num) % angle_den == 0:
        h = math.sqrt(0.5)
        cs, ss = (1 if c > 0 else -1), (1 if s > 0 else -1)
        if cs == ss:
            return ((x[0] - x[1]) * (h * cs), (x[0] + x[1]) * (h * cs))
        return ((x[0] + x[1]) * (h * cs), (x[1] - x[0]) * (h * cs))
    return (x[0] * c - x[1] * s, x[0] * s + x[1] * c)


def cfft(xs, sign):
    n = len(xs)
    if n == 1:
        return list(xs)
    if n == 2:
        return [cadd(xs[0], xs[1]), csub(xs[0], xs[1])]
    u = cfft(xs[0::2], sign)
    z = cfft(xs[1::4], sign)
    zp = cfft(xs[3::4], sign)
    out = [None] * n
    q = n // 4
    for k in range(q):
        a = cmul_const(z[k], sign * k, n)
        b = cmul_const(zp[k], sign * 3 * k, n)
        s = cadd(a, b)
        d = csub(a, b)
        t = (-d[1], d[0]) if sign > 0 else (d[1], -d[0])
        out[k] = cadd(u[k], s)
        out[k + 2 * q] = csub(u[k], s)
        out[k + q] = cadd(u[k + q], t)
        out[k + 3 * q] = csub(u[k + q], t)
    return out


def conj(x):
    return (x[0], -x[1])


def rfft(xs):
    n = len(xs)
    if n == 1:
        return [(xs[0], None)]
    if n == 2:
        return [(xs[0] + xs[1], None), (xs[0] - xs[1], None)]
    u = rfft(xs[0::2])
    z = rfft(xs[1::4])
    zp = rfft(xs[3::4])
    q = n // 4
    out = [None] * (n // 2 + 1)

    def bin_of(v, size, k):
        k = k % size
        if 2 * k <= size:
            return v[k]
        w = v[size - k]
        return w if w[1] is None else (w[0], -w[1])

    for k in range(q // 2 + 1):
        if k == 0:
            s = z[0][0] + zp[0][0]
            d = z[0][0] - zp[0][0]
            out[0] = (u[0][0] + s, None)
            out[2 * q] = (u[0][0] - s, None)
            out[q] = (u[q][0], -d)
            continue
        zk = bin_of(z, q, k)
        zpk = bin_of(zp, q, k)
        if zk[1] is None:
            zc = lambda v, num: (v * math.cos(2 * math.pi * num / n), v * math.sin(2 * math.pi * num / n))
            a = zc(zk[0], -k)
            b = zc(zpk[0], -3 * k)
        else:
            a = cmul_const(zk, -k, n)
            b = cmul_const(zpk, -3 * k, n)
        s = cadd(a, b)
        d = csub(a, b)
        uk = u[k] if u[k][1] is not None else (u[k][0], 0.0)
        uq = bin_of(u, 2 * q, k + q)
        uq = uq if uq[1] is not None else (uq[0], 0.0)
        out[k] = cadd(uk, s)
        out[2 * q - k] = (uk[0] - s[0], s[1] - uk[1])
        if k + q != 2 * q - k:
            out[q + k] = (uq[0] + d[1], uq[1] - d[0])
        if q - k != k:
            out[q - k] = (uq[0] - d[1], -(uq[1] + d[0]))
    return out


def c2r(hs, n):
    if n == 1:
        return [hs[0][0]]
    if n == 2:
        return [hs[0][0] + hs[1][0], hs[0][0] - hs[1][0]]
    half = n // 2
    even, odd = [], []
    for k in range(half // 2 + 1):
        a = hs[k]
        b = hs[half - k]
        if k == 0:
            even.append((a[0] + b[0], None))
            odd.append((a[0] - b[0], None))
        elif 2 * k == half:
            even.append((a[0] + a[0], None))
            odd.append((-(a[1] + a[1]), None))
        else:
            even.append((a[0] + b[0], a[1] - b[1]))
            odd.append(cmul_const((a[0] - b[0], a[1] + b[1]), k, n))
    e = c2r(even, half)
    o = c2r(odd, half)
    out = [None] * n
    out[0::2] = e
    out[1::2] = o
    return out


def split_bf(x):
    hi = x.astype(BF)
    lo = (x - hi.astype(F32)).astype(BF)
    return hi, lo


def mm(a, b):
    return jnp.dot(a, b, preferred_element_type=F32)


def np_split(t):
    t = np.asarray(t, np.float64)
    hi = t.astype(np.float32).astype(BF)
    lo = (t - hi.astype(np.float64)).astype(np.float32).astype(BF)
    return hi, lo


def phase(n, modulus):
    theta = 2.0 * np.pi * (np.asarray(n, np.int64) % modulus) / modulus
    return np.cos(theta), np.sin(theta)


def time_tables(samples, inner):
    outer = samples // inner
    b = np.arange(inner)[:, None]
    m = np.arange(inner // 2)[None, :]
    c, s = phase(b * m, inner)
    fwd = np.block([[c, -s], [s, c]])
    inv = np.block([[c.T, s.T], [-s.T, c.T]])
    k1 = np.arange(outer)[:, None]
    bb = np.arange(inner)[None, :]
    tc, ts = phase(k1 * bb, samples)
    return fwd, inv, tc.astype(np.float32), ts.astype(np.float32)


def chan_tables(channels, inner):
    outer = channels // inner
    q = np.arange(inner)[:, None]
    c0 = np.arange(inner)[None, :]
    c, s = phase(q * c0, inner)
    fwd = np.block([[c, s], [-s, c]])
    inv = np.block([[c.T, -s.T], [s.T, c.T]])
    p = np.arange(outer)[:, None]
    tc, ts = phase(p * np.arange(inner)[None, :], channels)
    return fwd, inv, tc.astype(np.float32), ts.astype(np.float32)


def time_forward(x, th, tl, tc, ts, inner, rows):
    row_count, samples = x.shape
    outer = samples // inner
    half = inner // 2
    tiles = inner // LANES
    sub = 16

    def body(x_ref, th_ref, tl_ref, tc_ref, ts_ref, o_ref, yh_ref, yl_ref):
        def group(g, carry):
            r0 = pl.multiple_of(g * sub, sub)
            for h in range(tiles):
                lanes = slice(h * LANES, (h + 1) * LANES)
                xs = [x_ref[pl.ds(r0, sub), a * inner + h * LANES : a * inner + (h + 1) * LANES] for a in range(outer)]
                ys = rfft(xs)
                for k in range(outer):
                    src = ys[k] if 2 * k <= outer else ys[outer - k]
                    neg = 2 * k > outer
                    c = tc_ref[k : k + 1, lanes]
                    s = ts_ref[k : k + 1, lanes]
                    if src[1] is None:
                        yr, yi = src[0] * c, -(src[0] * s)
                    elif neg:
                        yr = src[0] * c - src[1] * s
                        yi = -(src[0] * s + src[1] * c)
                    else:
                        yr = src[0] * c + src[1] * s
                        yi = src[1] * c - src[0] * s
                    rh, rl = split_bf(yr)
                    ih, il = split_bf(yi)
                    yh_ref[k, pl.ds(r0, sub), lanes] = rh
                    yl_ref[k, pl.ds(r0, sub), lanes] = rl
                    ilanes = slice(inner + h * LANES, inner + (h + 1) * LANES)
                    yh_ref[k, pl.ds(r0, sub), ilanes] = ih
                    yl_ref[k, pl.ds(r0, sub), ilanes] = il
            return carry

        lax.fori_loop(0, rows // sub, group, 0)
        per = 8

        def product(g, carry):
            k0 = pl.multiple_of(g * per, per)
            yh = yh_ref[pl.ds(k0, per)].reshape(per * rows, 2 * inner)
            yl = yl_ref[pl.ds(k0, per)].reshape(per * rows, 2 * inner)
            z = mm(yh, th_ref[...]) + mm(yl, th_ref[...]) + mm(yh, tl_ref[...])
            z = z.astype(BF).reshape(per, rows, 2 * half)
            o_ref[pl.ds(k0, per), 0] = z[:, :, :half]
            o_ref[pl.ds(k0, per), 1] = z[:, :, half:]
            return carry

        lax.fori_loop(0, outer // per, product, 0)

    full = lambda a: pl.BlockSpec(a.shape, lambda i: (0,) * a.ndim)
    return pl.pallas_call(
        body,
        grid=(row_count // rows,),
        in_specs=[pl.BlockSpec((rows, samples), lambda i: (i, 0)), full(th), full(tl), full(tc), full(ts)],
        out_specs=pl.BlockSpec((outer, 2, rows, half), lambda i: (0, 0, i, 0)),
        out_shape=jax.ShapeDtypeStruct((outer, 2, row_count, half), BF),
        scratch_shapes=[pltpu.VMEM((outer, rows, 2 * inner), BF)] * 2,
        compiler_params=pltpu.CompilerParams(vmem_limit_bytes=VMEM_BYTES),
        name="time_forward",
    )(x, th, tl, tc, ts)


def channel_filter(z, limit, weight, fh, fl, gh, gl, tc, ts, inner):
    peers, own, _, row_count, bins = z.shape
    channels = peers * row_count
    outer = channels // inner
    per_peer = row_count // inner
    sub = 16

    def body(z_ref, lim_ref, wt_ref, fh_ref, fl_ref, gh_ref, gl_ref, tc_ref, ts_ref, o_ref, v_ref, w_ref):
        def fwd(g, carry):
            r0 = pl.multiple_of(g * sub, sub)
            xs = []
            for c1 in range(outer):
                peer, part = c1 // per_peer, c1 % per_peer
                rr = pl.ds(part * inner + r0, sub)
                xs.append((z_ref[peer, 0, 0, rr, :].astype(F32), z_ref[peer, 0, 1, rr, :].astype(F32)))
            vs = cfft(xs, -1)
            for p in range(outer):
                c = tc_ref[p, pl.ds(r0, sub), :]
                s = ts_ref[p, pl.ds(r0, sub), :]
                vr, vi = vs[p]
                rh, rl = split_bf(vr * c + vi * s)
                ih, il = split_bf(vi * c - vr * s)
                v_ref[p, pl.ds(r0, sub), :bins] = rh
                v_ref[p, pl.ds(r0, sub), bins:] = rl
                v_ref[p, pl.ds(inner + r0, sub), :bins] = ih
                v_ref[p, pl.ds(inner + r0, sub), bins:] = il
            return carry

        lax.fori_loop(0, inner // sub, fwd, 0)
        limit_row = lim_ref[0]
        weight_row = wt_ref[0]
        q_index = lax.broadcasted_iota(jnp.int32, (inner, bins), 0)

        def middle(p, carry):
            v = v_ref[p]
            u2 = mm(fh_ref[...], v)
            u = u2[:, :bins] + u2[:, bins:] + mm(fl_ref[...], v[:, :bins])
            kc = p + outer * q_index
            kc = jnp.where(kc < channels // 2, kc, channels - kc)
            gain = jnp.where(kc <= limit_row, weight_row, 0.0)
            uh, ul = split_bf(jnp.concatenate([u[:inner] * gain, u[inner:] * gain], axis=0))
            w2 = mm(gh_ref[...], jnp.concatenate([uh, ul], axis=1))
            w = w2[:, :bins] + w2[:, bins:] + mm(gl_ref[...], uh)
            c = tc_ref[p]
            s = ts_ref[p]
            wr, wi = w[:inner], w[inner:]
            w_ref[p, 0] = wr * c - wi * s
            w_ref[p, 1] = wr * s + wi * c
            return carry

        lax.fori_loop(0, outer, middle, 0, unroll=2)

        def back(g, carry):
            r0 = pl.multiple_of(g * sub, sub)
            ws = [(w_ref[p, 0, pl.ds(r0, sub), :], w_ref[p, 1, pl.ds(r0, sub), :]) for p in range(outer)]
            ys = cfft(ws, 1)
            for c1 in range(outer):
                peer, part = c1 // per_peer, c1 % per_peer
                rr = pl.ds(part * inner + r0, sub)
                o_ref[peer, 0, 0, rr, :] = ys[c1][0].astype(BF)
                o_ref[peer, 0, 1, rr, :] = ys[c1][1].astype(BF)
            return carry

        lax.fori_loop(0, inner // sub, back, 0)

    full = lambda a: pl.BlockSpec(a.shape, lambda i: (0,) * a.ndim)
    block = pl.BlockSpec((peers, 1, 2, row_count, bins), lambda i: (0, i, 0, 0, 0))
    row = pl.BlockSpec((1, 1, bins), lambda i: (i, 0, 0))
    return pl.pallas_call(
        body,
        grid=(own,),
        in_specs=[block, row, row, full(fh), full(fl), full(gh), full(gl), full(tc), full(ts)],
        out_specs=block,
        out_shape=jax.ShapeDtypeStruct(z.shape, BF),
        scratch_shapes=[
            pltpu.VMEM((outer, 2 * inner, 2 * bins), BF),
            pltpu.VMEM((outer, 2, inner, bins), F32),
        ],
        compiler_params=pltpu.CompilerParams(vmem_limit_bytes=VMEM_BYTES),
        name="channel_filter",
    )(z, limit, weight, fh, fl, gh, gl, tc, ts)


def time_inverse(h, th, tl, tc, ts, inner, rows):
    outer, _, row_count, half = h.shape
    samples = outer * inner
    tiles = inner // LANES
    sub = 8

    def body(h_ref, th_ref, tl_ref, tc_ref, ts_ref, o_ref, low_ref, g_ref):
        per = 8

        def product(g, carry):
            k0 = pl.multiple_of(g * per, per)
            hr = h_ref[pl.ds(k0, per), 0].reshape(per * rows, half)
            hi = h_ref[pl.ds(k0, per), 1].reshape(per * rows, half)
            hh = jnp.concatenate([hr, hi], axis=1)
            w = mm(hh, th_ref[...]) + mm(hh, tl_ref[...])
            g_ref[pl.ds(k0, per)] = w.reshape(per, rows, 2 * inner)
            return carry

        lax.fori_loop(0, outer // per, product, 0)

        def group(g, carry):
            r0 = pl.multiple_of(g * sub, sub)
            for t in range(tiles):
                lanes = slice(t * LANES, (t + 1) * LANES)
                ilanes = slice(inner + t * LANES, inner + (t + 1) * LANES)
                gs = []
                for k in range(outer):
                    wr = g_ref[k, pl.ds(r0, sub), lanes]
                    wi = g_ref[k, pl.ds(r0, sub), ilanes]
                    c = tc_ref[k : k + 1, lanes]
                    s = ts_ref[k : k + 1, lanes]
                    gs.append((wr * c - wi * s, wr * s + wi * c))
                hs = []
                for k in range(outer // 2 + 1):
                    a, b = gs[k], gs[(outer - k) % outer]
                    hs.append((a[0] + b[0], a[1] - b[1]))
                xs = c2r(hs, outer)
                for a in range(outer):
                    cols = slice(a * inner + t * LANES, a * inner + (t + 1) * LANES)
                    o_ref[pl.ds(r0, sub), cols] = xs[a]
            return carry

        lax.fori_loop(0, rows // sub, group, 0)
        low_ref[...] = o_ref[...].astype(BF)

    full = lambda a: pl.BlockSpec(a.shape, lambda i: (0,) * a.ndim)
    out_block = pl.BlockSpec((rows, samples), lambda i: (i, 0))
    return pl.pallas_call(
        body,
        grid=(row_count // rows,),
        in_specs=[pl.BlockSpec((outer, 2, rows, half), lambda i: (0, 0, i, 0)), full(th), full(tl), full(tc), full(ts)],
        out_specs=[out_block, out_block],
        out_shape=[
            jax.ShapeDtypeStruct((row_count, samples), F32),
            jax.ShapeDtypeStruct((row_count, samples), BF),
        ],
        scratch_shapes=[pltpu.VMEM((outer, rows, 2 * inner), F32)],
        compiler_params=pltpu.CompilerParams(vmem_limit_bytes=VMEM_BYTES),
        name="time_inverse",
    )(h, th, tl, tc, ts)


def window_energy(low, stack, step):
    depth, samples = low.shape
    width = stack.shape[1]
    windows = samples // WIN
    per_step = step // WIN
    chunk = 256

    def body(low_ref, st_ref, o_ref, e_ref):
        i = pl.program_id(0)
        lt = low_ref[...].T
        for n in range(width // chunk):
            cols = slice(n * chunk, (n + 1) * chunk)
            d = mm(lt, st_ref[:, cols])
            sq = d * d
            e_ref[pl.ds(pl.multiple_of(i * per_step, per_step), per_step), cols] = jnp.sum(
                sq.reshape(per_step, WIN, chunk), axis=1
            ) * (1.0 / WIN)

        @pl.when(i == pl.num_programs(0) - 1)
        def _():
            for n in range(width // chunk):
                cols = slice(n * chunk, (n + 1) * chunk)
                o_ref[cols, :] = e_ref[:, cols].T

    return pl.pallas_call(
        body,
        grid=(samples // step,),
        in_specs=[pl.BlockSpec((depth, step), lambda i: (0, i)), pl.BlockSpec(stack.shape, lambda i: (0, 0))],
        out_specs=pl.BlockSpec((width, windows), lambda i: (0, 0)),
        out_shape=jax.ShapeDtypeStruct((width, windows), F32),
        scratch_shapes=[pltpu.VMEM((windows, width), F32)],
        compiler_params=pltpu.CompilerParams(vmem_limit_bytes=VMEM_BYTES),
        name="window_energy",
    )(low, stack)


def toeplitz(kernel_low, depth, count):
    templates, span = kernel_low.shape
    u = jnp.pad(kernel_low, ((0, 0), (1, depth + 1 - 1 - span)))
    flat = jnp.tile(u, (1, count))[:, : count * depth]
    m = flat.reshape(templates, count, depth)
    return jnp.transpose(m, (2, 1, 0)).reshape(depth, count * templates)


def per_device(das_window, fan_bound, tap_offset, tap_weight):
    row_count, samples = das_window.shape
    devices = lax.axis_size("chan")
    channels = row_count * devices
    inner = 256
    outer = samples // inner
    half = inner // 2
    own = outer // devices
    chan_inner = 128
    chan_outer = channels // chan_inner
    assert outer % devices == 0 and row_count % chan_inner == 0

    t_fwd, t_inv, ttc, tts = time_tables(samples, inner)
    back_scale = 0.125
    tfh, tfl = np_split(t_fwd)
    tih, til = np_split(t_inv * (1.0 / (samples * back_scale)))
    ttc, tts = jnp.asarray(ttc), jnp.asarray(tts)
    c_fwd, c_inv, ctc, cts = chan_tables(channels, chan_inner)
    cfh, cfl = np_split(c_fwd)
    cgh, cgl = np_split(c_inv)

    spectrum = time_forward(das_window, jnp.asarray(tfh), jnp.asarray(tfl), ttc, tts, inner, 32)
    spectrum = spectrum.reshape(devices, own, 2, row_count, half)
    by_freq = lax.all_to_all(spectrum, "chan", split_axis=0, concat_axis=0, tiled=True)

    position = lax.axis_index("chan")
    by_outer = jnp.transpose(fan_bound.reshape(half, outer), (1, 0))
    limit = lax.dynamic_slice_in_dim(by_outer, position * own, own, 0).reshape(own, 1, half)
    bin_outer = lax.broadcasted_iota(jnp.int32, (own, 1, half), 0) + position * own
    bin_inner = lax.broadcasted_iota(jnp.int32, (own, 1, half), 2)
    scale = back_scale / channels
    weight = jnp.where(bin_outer + bin_inner == 0, 0.5 * scale, scale).astype(F32)
    ctw = jnp.broadcast_to(jnp.asarray(ctc)[:, :, None], (chan_outer, chan_inner, half))
    stw = jnp.broadcast_to(jnp.asarray(cts)[:, :, None], (chan_outer, chan_inner, half))
    back = channel_filter(
        by_freq, limit, weight, jnp.asarray(cfh), jnp.asarray(cfl), jnp.asarray(cgh), jnp.asarray(cgl), ctw, stw, chan_inner
    )
    by_channel = lax.all_to_all(back, "chan", split_axis=0, concat_axis=0, tiled=True)
    by_channel = by_channel.reshape(outer, 2, row_count, half)
    filtered, low = time_inverse(by_channel, jnp.asarray(tih), jnp.asarray(til), ttc, tts, inner, 32)

    up = [(i, i + 1) for i in range(devices - 1)]
    down = [(i + 1, i) for i in range(devices - 1)]
    before = lax.ppermute(low[row_count - EDGE :], "chan", up)
    after = lax.ppermute(low[:EDGE], "chan", down)

    offsets_grid = jnp.arange(2 * HALO + 1, dtype=jnp.int32) - HALO
    matches = (tap_offset[:, :, None] == offsets_grid[None, None, :]).astype(F32)
    kernel_low = jnp.sum(tap_weight[:, :, None] * matches, axis=1).astype(BF)
    templates = kernel_low.shape[0]
    inside = toeplitz(kernel_low, row_count, row_count - 2 * EDGE)
    edge = toeplitz(kernel_low, 3 * EDGE, EDGE)
    edges = jnp.concatenate(
        [jnp.pad(edge, ((0, 0), (0, edge.shape[1]))), jnp.pad(edge, ((0, 0), (edge.shape[1], 0)))], axis=0
    )
    e_in = window_energy(low, inside, 512)
    ends = jnp.concatenate([before, low[: 2 * EDGE], low[row_count - 2 * EDGE :], after], axis=0)
    e_out = window_energy(ends, edges, 512)
    windows = samples // WIN
    cut = EDGE * templates
    energy = jnp.concatenate([e_out[:cut], e_in, e_out[cut:]], axis=0)
    return filtered, energy.reshape(row_count, templates, windows)


def solution(mesh):
    return jax.shard_map(
        per_device,
        mesh=mesh,
        in_specs=(P(("survey", "chan"), None), P(), P(), P()),
        out_specs=(P(("survey", "chan"), None), P(("survey", "chan"), None, None)),
        check_vma=False,
    )
```

time: 750 us -> 316 us (0.42)
  matrix products: 184 us -> 0 us
  waiting for transfers between devices: 344 us -> 178 us
  local copies, waits for them, and re-layouts: 120 us -> 12.5 us
  Pallas kernels: 0 us -> 101 us
  other arithmetic: 67 us -> 4.35 us
  loops' own time: 7.54 us -> 0 us
    dot_general x13 -> x0, matrix products: 184 us -> none  [the longest x2 44.2 us: channel_transform(): out = jnp.einsum('kbpn,pkbqm->mkqn', first, second_table, precision=PRECISE)]
    all_to_all x2, waiting for transfers between devices: 332 us -> 178 us  [the longest x1 90.6 us: per_device(): lax.all_to_all(spectrum, 'chan', split_axis=0, concat_axis=0, tiled=True)]
    pallas_call x0 -> x5, Pallas kernels: none -> 101 us  [the longest x1 35.7 us: channel_filter(): pl.pallas_call(body, grid=(own,), in_specs=[block, row, row, full(fh), fu...]
    all_to_all x4 -> x0, local copies, waits for them, and re-layouts: 32.3 us -> none  [the longest x2 16.2 us: per_device(): lax.all_to_all(spectrum, 'chan', split_axis=2, concat_axis=0, tiled=True)]
    div x6 -> x0, local copies, waits for them, and re-layouts: 28.8 us -> none  [the longest x2 28.3 us: per_device(): back = channel_transform(wave * passing[:, None, :], 1.0) / channel_count]
    reshape x1 -> x4, local copies, waits for them, and re-layouts: 23.4 us -> 1.45 us  [the longest x2 1.25 us: toeplitz(): return jnp.transpose(m, (2, 1, 0)).reshape(depth, count * templates)]
    transpose x2, local copies, waits for them, and re-layouts: 21.7 us -> 0.47 us  [toeplitz(): return jnp.transpose(m, (2, 1, 0)).reshape(depth, count * templates)]
    mul x5 -> x0, other arithmetic: 17.1 us -> none  [the longest x3 17.1 us: phases(): return (jnp.cos(angle), direction * jnp.sin(angle))]
  transfers between devices with their start and end apart: 4 -> 4, of which waited for: 4 -> 2; matrix products, arithmetic and copies ran while one was open for 4% -> 2% of each run, Pallas kernels for 0% -> 5%
where the time goes in v1:
time: 316 us; the launch traced here: 313 us
  waiting for transfers between devices  178 us (56%)
  Pallas kernels  101 us (32%)
  starting transfers between devices  16.7 us (5%)
  local copies, waits for them, and re-layouts  12.5 us (4%)
  other arithmetic  4.35 us (1%)
    all_to_all x1, waiting for transfers between devices, per_device(): lax.all_to_all(spectrum, 'chan', split_axis=0, concat_axis=0, tiled=True)  90.6 us
    all_to_all x1, waiting for transfers between devices, per_device(): lax.all_to_all(back, 'chan', split_axis=0, concat_axis=0, tiled=True)  87.4 us
    pallas_call x1, Pallas kernels, channel_filter(): pl.pallas_call(body, grid=(own,), in_specs=[block, row, row, full(fh), fu...  35.7 us
    pallas_call x2, Pallas kernels, window_energy(): pl.pallas_call(body, grid=(samples // step,), in_specs=[pl.BlockSpec((dep...  26.4 us
    pallas_call x1, Pallas kernels, time_forward(): pl.pallas_call(body, grid=(row_count // rows,), in_specs=[pl.BlockSpec((r...  20.8 us
    pallas_call x1, Pallas kernels, time_inverse(): pl.pallas_call(body, grid=(row_count // rows,), in_specs=[pl.BlockSpec((o...  17.7 us
    all_to_all x1, starting transfers between devices, per_device(): lax.all_to_all(spectrum, 'chan', split_axis=0, concat_axis=0, tiled=True)  6.61 us
  transfers between devices with their start and end apart: 4, of which 2 were waited for; matrix products, arithmetic and copies ran while one was open for 2% of the time, Pallas kernels for 5%

profile of v1, /device:TPU:19, one launch (start us, length us, event | category | flops | bytes accessed | tf_op | source)
XLA Modules:
  0.0 312.9 jit_solution(7065339108839239349)
XLA Ops:
  0.6 20.8 %time_forward.1 = bf16[32,2,256,128]{3,2,1,0:T(8,128)(2,1)} custom-call(f32[256,8192]{1,0:T(8,128)} %x_ref.1, bf16[512,256]{1,0:T(8,128)(2,1)} %constant.49.clone.th_ref, bf16[512,256]{1,0:T(8,128)(2,1)} %constant.50.clone.tl_ref, f32[32,256]{1,0:T(8,128)} %constant.47.clone.tc_ref, f32[32,256]{1,0:T(8,128)} %constant.48.clone.ts_ref), custom_call_target="tpu_custom_call" | custom-call | tf_op jit(solution)/shard_map/time_forward/pallas_call | solution.py:252
  21.5 6.6 %all-to-all-start = ((bf16[16,2,2,256,128]{4,3,2,1,0:T(8,128)(2,1)}), bf16[16,2,2,256,128]{4,3,2,1,0:T(8,128)(2,1)}, u32[]{:S(2)}, u32[]{:S(2)}) async-start(bf16[16,2,2,256,128]{4,3,2,1,0:T(8,128)(2,1)} %bitcast.21), calls=%async_computation | async-start | bytes 8388608 | tf_op jit(solution)/shard_map/all_to_all | solution.py:476
  28.2 0.1 constant_dynamic-slice_fusion
  28.2 0.7 copy.30
  28.9 0.6 compare_select_fusion.wt_ref
  29.6 90.6 %all-to-all-done.z_ref = bf16[16,2,2,256,128]{4,3,2,1,0:T(8,128)(2,1)} async-done(((bf16[16,2,2,256,128]{4,3,2,1,0:T(8,128)(2,1)}), bf16[16,2,2,256,128]{4,3,2,1,0:T(8,128)(2,1)}, u32[]{:S(2)}, u32[]{:S(2)}) %all-to-all-start) | async-done | bytes 4194336 | tf_op jit(solution)/shard_map/all_to_all | solution.py:476
  120.2 1.9 broadcast_in_dim.14.tc_ref
  122.1 1.9 broadcast_in_dim.26.ts_ref
  124.1 35.7 %channel_filter.1 = bf16[16,2,2,256,128]{4,3,2,1,0:T(8,128)(2,1)} custom-call(bf16[16,2,2,256,128]{4,3,2,1,0:T(8,128)(2,1)} %all-to-all-done.z_ref, s32[2,1,128]{2,1,0:T(1,128)} %bitcast.27, f32[2,1,128]{2,1,0:T(1,128)} %compare_select_fusion.wt_ref, bf16[256,256]{1,0:T(8,128)(2,1)} %constant.53.clone.fh_ref, bf16[256,256]{1,0:T(8,128)(2,1)} %constant.54.clone.fl_ref, ...), custom_call_target="tpu_custom_call" | custom-call | tf_op jit(solution)/shard_map/channel_filter/pallas_call | solution.py:332
  159.8 5.3 %all-to-all-start.1 = ((bf16[16,2,2,256,128]{4,3,2,1,0:T(8,128)(2,1)}), bf16[16,2,2,256,128]{4,3,2,1,0:T(8,128)(2,1)}, u32[]{:S(2)}, u32[]{:S(2)}) async-start(bf16[16,2,2,256,128]{4,3,2,1,0:T(8,128)(2,1)} %channel_filter.1), calls=%async_computation.1 | async-start | bytes 8388608 | tf_op jit(solution)/shard_map/all_to_all | solution.py:490
  165.1 0.1 select_reduce_fusion
  165.2 0.1 pad.16
  165.4 0.1 tile.9
  165.6 0.1 reshape.83
  165.7 0.1 copy.26
  165.8 0.1 tile.20
  166.0 1.3 tile.21
  167.3 0.2 copy.35
  167.5 0.4 copy.36
  167.9 1.2 copy.29.st_ref
  169.1 0.7 fusion.2.st_ref
  169.8 87.4 %all-to-all-done.1 = bf16[16,2,2,256,128]{4,3,2,1,0:T(8,128)(2,1)} async-done(((bf16[16,2,2,256,128]{4,3,2,1,0:T(8,128)(2,1)}), bf16[16,2,2,256,128]{4,3,2,1,0:T(8,128)(2,1)}, u32[]{:S(2)}, u32[]{:S(2)}) %all-to-all-start.1) | async-done | bytes 4194336 | tf_op jit(solution)/shard_map/all_to_all | solution.py:490
  257.1 17.7 %time_inverse.1 = (f32[256,8192]{1,0:T(8,128)}, bf16[256,8192]{1,0:T(8,128)(2,1)}) custom-call(bf16[32,2,256,128]{3,2,1,0:T(8,128)(2,1)} %bitcast.3.h_ref, bf16[256,512]{1,0:T(8,128)(2,1)} %constant.57.clone.th_ref, bf16[256,512]{1,0:T(8,128)(2,1)} %constant.58.clone.tl_ref, f32[32,256]{1,0:T(8,128)} %constant.47.clone.tc_ref, f32[32,256]{1,0:T(8,128)} %constant.48.clone.ts_ref), custom_call_target="tpu_custom_call" | custom-call | tf_op jit(solution)/shard_map/time_inverse/pallas_call | solution.py:394
  274.8 1.3 fusion.3
  276.1 2.1 collective-permute-start
  278.2 2.7 collective-permute-start.1
  280.9 1.7 fusion.4
  282.6 14.8 %window_energy.3 = f32[1536,128]{1,0:T(8,128)} custom-call(bf16[256,8192]{1,0:T(8,128)(2,1)} %get-tuple-element.5.low_ref, bf16[256,1536]{1,0:T(8,128)(2,1)} %copy.29.st_ref), custom_call_target="tpu_custom_call" | custom-call | tf_op jit(solution)/shard_map/window_energy/pallas_call | solution.py:433
  297.4 1.8 pad_maximum_fusion.low_ref
  299.2 11.7 %window_energy.2 = f32[512,128]{1,0:T(8,128)} custom-call(bf16[192,8192]{1,0:T(8,128)(2,1)} %pad_maximum_fusion.low_ref, bf16[192,512]{1,0:T(8,128)(2,1)} %fusion.2.st_ref), custom_call_target="tpu_custom_call" | custom-call | tf_op jit(solution)/shard_map/window_energy/pallas_call | solution.py:433
  310.9 1.0 fusion.5
  311.9 1.0 maximum_bitcast_fusion
  (22 shorter events, 0.3 us)
Async XLA Ops:
  21.5 6.6 %copy-start.3 = (s32[4096]{0:T(1024)S(1)}, s32[4096]{0:T(1024)}, u32[]{:S(2)}) copy-start(s32[4096]{0:T(1024)} %param.17) | copy-start | bytes 49156
  21.5 98.7 %copy-start.2 = (f32[32,128]{1,0:T(8,128)S(1)}, f32[32,128]{1,0:T(8,128)}, u32[]{:S(2)}) copy-start(f32[32,128]{1,0:T(8,128)} %constant.51.clone) | copy-start | bytes 49156
  21.5 100.6 %copy-start.1 = (f32[32,128]{1,0:T(8,128)S(1)}, f32[32,128]{1,0:T(8,128)}, u32[]{:S(2)}) copy-start(f32[32,128]{1,0:T(8,128)} %constant.52.clone) | copy-start | bytes 49156
  21.5 98.7 %all-to-all-start = ((bf16[16,2,2,256,128]{4,3,2,1,0:T(8,128)(2,1)}), bf16[16,2,2,256,128]{4,3,2,1,0:T(8,128)(2,1)}, u32[]{:S(2)}, u32[]{:S(2)}) async-start(bf16[16,2,2,256,128]{4,3,2,1,0:T(8,128)(2,1)} %bitcast.21), calls=%async_computation | async-start | bytes 8388608 | tf_op jit(solution)/shard_map/all_to_all | solution.py:476
  159.7 5.3 %copy-start.4 = (f32[8,32]{1,0:T(8,128)S(1)}, f32[8,32]{1,0:T(8,128)}, u32[]{:S(2)}) copy-start(f32[8,32]{1,0:T(8,128)} %param.19) | copy-start | bytes 3076
  159.8 5.3 %copy-start.5 = (s32[8,32]{1,0:T(8,128)S(1)}, s32[8,32]{1,0:T(8,128)}, u32[]{:S(2)}) copy-start(s32[8,32]{1,0:T(8,128)} %param.18) | copy-start | bytes 3076
  159.8 97.4 %all-to-all-start.1 = ((bf16[16,2,2,256,128]{4,3,2,1,0:T(8,128)(2,1)}), bf16[16,2,2,256,128]{4,3,2,1,0:T(8,128)(2,1)}, u32[]{:S(2)}, u32[]{:S(2)}) async-start(bf16[16,2,2,256,128]{4,3,2,1,0:T(8,128)(2,1)} %channel_filter.1), calls=%async_computation.1 | async-start | bytes 8388608 | tf_op jit(solution)/shard_map/all_to_all | solution.py:490
  276.1 21.3 %collective-permute-start = (bf16[32,8192]{1,0:T(8,128)(2,1)S(1)}, bf16[32,8192]{1,0:T(8,128)(2,1)S(1)}, u32[]{:S(2)}, u32[]{:S(2)}) collective-permute-start(bf16[32,8192]{1,0:T(8,128)(2,1)S(1)} %get-tuple-element.6), channel_id=1, source_target_pairs={{0,1},{1,2},{2,3},{3,4},{4,5},{5,6},{6,7},{7,8},{8,9},{9,10},{10,1... | collective-permute-start | bytes 1572872 | tf_op jit(solution)/shard_map/ppermute | solution.py:496
  278.2 19.2 %collective-permute-start.1 = (bf16[32,8192]{1,0:T(8,128)(2,1)S(1)}, bf16[32,8192]{1,0:T(8,128)(2,1)S(1)}, u32[]{:S(2)}, u32[]{:S(2)}) collective-permute-start(bf16[32,8192]{1,0:T(8,128)(2,1)S(1)} %get-tuple-element.7), channel_id=1, source_target_pairs={{1,0},{2,1},{3,2},{4,3},{5,4},{6,5},{7,6},{8,7},{9,8},{10,9},{11,1... | collective-permute-start | bytes 1572872 | tf_op jit(solution)/shard_map/ppermute | solution.py:497
  297.4 14.5 %copy-start = (f32[1536,128]{1,0:T(8,128)S(1)}, f32[1536,128]{1,0:T(8,128)}, u32[]{:S(2)}) copy-start(f32[1536,128]{1,0:T(8,128)} %window_energy.3) | copy-start | bytes 2359300
